TPU v7x, 512 devices: a whole 4x8x8 slice. The times are simulated.
512 devices in a mesh: context: 32 (over y, x), tensor: 16 (over z, core).
Axes of the slice: x: 4, y: 8, z: 8, core: 2. Of those that a mesh axis runs over, the one named last changes fastest.
Arguments:
- queries: bfloat16 [1, 16384, 4096], P(None, 'context', 'tensor'), may hold values from -6 to 6
- keys: bfloat16 [1, 16384, 4096], P(None, 'context', 'tensor'), may hold values from -0.546875 to 0.546875
- spike_counts: int32 [1, 16384, 4096], P(None, 'context', 'tensor'), may hold values from -4 to 4
- spike_scale: float32 [4096], P('tensor'), may hold values from 0.5 to 2
- log_decay: float32 [1, 32, 16384], P(None, 'tensor', 'context'), may hold values from -3 to 0, as said below
- norm_gain: float32 [4096], P('tensor'), may hold values from 0.5 to 1.5
- out_weight: bfloat16 [4096, 8192], P('context', 'tensor'), may hold values from -0.09375 to 0.09375
- residual_in: bfloat16 [1, 16384, 8192], P(None, 'context', 'tensor'), may hold values from -6 to 6
Outputs:
- residual_out: bfloat16 [1, 16384, 8192], P(None, 'context', 'tensor')
Inputs may be any that keep to these rules, and one draw needn't show every extreme that they name: log_decay is negative.
All inputs are finite; a program needn't handle non-finite values.
Results may differ from a plain program's by a relative error of at most 0.0095.
Values may be sent and summed in bfloat16 or wider, within the bound.
A program may use at most 64 MiB of HBM per device.

v0:
```python
import jax
import jax.numpy as jnp
from jax import lax
from jax.sharding import PartitionSpec as P

epsilon = 1e-06


def prefix_2(value, axis, combine, identity):
    size, position = (lax.axis_size(axis), lax.axis_index(axis))
    everything = jax.tree.map(
        lambda part, kind: lax.all_gather(part.astype(kind), axis),
        value,
        (jnp.bfloat16, jnp.bfloat16),
    )
    start = jax.tree.map(
        lambda part, zero: jnp.broadcast_to(jnp.asarray(zero, part.dtype), part.shape),
        value,
        identity,
    )

    def lap(k, before):
        reached = k < position
        new = combine(
            before, jax.tree.map(lambda part, own: part[k].astype(own.dtype), everything, value)
        )
        return jax.tree.map(lambda a, b: jnp.where(reached, a, b), new, before)

    return lax.fori_loop(0, size, lap, start)


def combine(earlier, later):
    return (earlier[0] * later[0], later[0][..., None, None] * earlier[1] + later[1])


def local(queries, keys, spike_counts, spike_scale, log_decay, norm_gain, out_weight, residual_in):
    requests, block, width_here = queries.shape
    heads = log_decay.shape[1]
    head_size = width_here // heads
    values = (spike_counts.astype(jnp.float32) * spike_scale).astype(jnp.bfloat16)

    def split_heads(array):
        return array.reshape(requests, block, heads, head_size).transpose(0, 2, 1, 3)

    query_h = split_heads(queries)
    key_h = split_heads(keys)
    value_h = split_heads(values)
    cumulative = jnp.cumsum(log_decay, axis=2)
    vocabulary_identifiers = jnp.arange(block)
    causal = vocabulary_identifiers[:, None] >= vocabulary_identifiers[None, :]
    gaps = cumulative[..., :, None] - cumulative[..., None, :]
    decay_mat = jnp.exp(jnp.where(causal, gaps, -1e30))
    scores = jnp.einsum("rhtd,rhsd->rhts", query_h, key_h, preferred_element_type=jnp.float32)
    weights = (scores * decay_mat).astype(jnp.bfloat16)
    intra = jnp.einsum("rhts,rhsd->rhtd", weights, value_h, preferred_element_type=jnp.float32)
    to_end = jnp.exp(cumulative[..., -1:] - cumulative)
    weighted_keys = (key_h.astype(jnp.float32) * to_end[..., None]).astype(jnp.bfloat16)
    own_state = jnp.einsum(
        "rhsd,rhse->rhde", weighted_keys, value_h, preferred_element_type=jnp.float32
    )
    span_decay = jnp.exp(cumulative[..., -1])
    prefix = prefix_2(
        (span_decay, own_state),
        "context",
        combine,
        (jnp.ones_like(span_decay), jnp.zeros_like(own_state)),
    )
    incoming = prefix[1]
    carried = jnp.exp(cumulative)[..., None] * jnp.einsum(
        "rhtd,rhde->rhte", query_h.astype(jnp.float32), incoming, precision=lax.Precision.HIGHEST
    )
    mixed = intra + carried
    scale = lax.rsqrt(jnp.mean(mixed * mixed, axis=-1, keepdims=True) + epsilon)
    normed = (mixed * scale * norm_gain.reshape(1, heads, 1, head_size)).astype(jnp.bfloat16)
    normed = normed.transpose(0, 2, 1, 3).reshape(requests * block, width_here)
    all_heads = lax.all_gather(normed, "tensor", axis=1, tiled=True)
    projected = jnp.dot(
        all_heads,
        lax.all_gather(out_weight, "context", axis=0, tiled=True),
        preferred_element_type=jnp.float32,
    )
    projected = projected.reshape(requests, block, out_weight.shape[1])
    return (residual_in.astype(jnp.float32) + projected).astype(jnp.bfloat16)


def solution(mesh):
    in_specs = (
        P(None, "context", "tensor"),
        P(None, "context", "tensor"),
        P(None, "context", "tensor"),
        P("tensor"),
        P(None, "tensor", "context"),
        P("tensor"),
        P("context", "tensor"),
        P(None, "context", "tensor"),
    )
    out_specs = P(None, "context", "tensor")
    return jax.shard_map(local, mesh=mesh, in_specs=in_specs, out_specs=out_specs, check_vma=False)
```

profile of v0, /device:TPU:1, one launch (start us, length us, event | category | flops | bytes accessed | tf_op | source)
XLA Modules:
  0.0 247.4 jit_solution(11480079209673487597)
XLA Ops:
  8.4 1.1 copy.44
  9.5 1.1 multiply_convert_fusion.3
  12.7 31.4 %all-gather = bf16[32,2,1]{2,1,0:T(2,128)(2,1)S(1)} all-gather(bf16[1,2,1]{2,1,0:T(2,128)(2,1)S(1)} %get-tuple-element.154), channel_id=2, replica_groups=mesh['context'=32,'tensor'=16] {'context'}, dimensions={0}, use_global_device_ids=true | all-gather | bytes 132 | tf_op jit(solution)/shard_map/all_gather | solution.py:12
  44.3 52.7 %all-gather.10.cloned.1.call-done = bf16[64,128,128]{2,1,0:T(8,128)(2,1)} async-done(((bf16[2,128,128]{2,1,0:T(8,128)(2,1)}), bf16[64,128,128]{2,1,0:T(8,128)(2,1)}) %all-gather.10.cloned.1.call-update) | async-done | bytes 2097168 | tf_op jit(solution)/shard_map/all_gather | solution.py:12
  97.0 36.8 %while.14 = (s32[]{:T(128)}, f32[1,2,128,128]{3,2,1,0:T(8,128)S(1)}, s32[]{:T(128)}, bf16[32,1,2]{0,2,1:T(2,128)(2,1)S(1)}, bf16[32,1,2,128,128]{4,3,2,1,0:T(8,128)(2,1)}, /*index=5*/s32[]{:T(128)}, s32[]{:T(128)}) while((s32[]{:T(128)}, f32[1,2,128,128]{3,2,1,0:T(8,128)S(1)}, s32[]{:T(128)}, bf16[32,1,2]{0,2,1:T(2,128)(2,1)S(1)}, ...), condition=%wide.region_3.4_spmd.clone, body=%wide.region_2.3_spmd.clone.sunk | while | flops 163846 | bytes 327829 | solution.py:29
  98.3 0.9 fusion.25
  99.5 0.9 fusion.25
  100.6 0.9 fusion.25
  101.8 0.9 fusion.25
  102.9 0.9 fusion.25
  104.1 0.9 fusion.25
  105.2 0.9 fusion.25
  106.4 0.9 fusion.25
  107.5 0.9 fusion.25
  108.7 0.9 fusion.25
  109.8 0.9 fusion.25
  111.0 0.9 fusion.25
  112.1 0.9 fusion.25
  113.3 0.9 fusion.25
  114.4 0.9 fusion.25
  115.6 0.9 fusion.25
  116.7 0.9 fusion.25
  119.0 0.9 fusion.25
  121.3 0.9 fusion.25
  122.5 0.9 fusion.25
  124.8 0.9 fusion.25
  128.2 0.9 fusion.25
  130.5 0.9 fusion.25
  134.2 1.0 multiply_reduce_fusion
  136.1 49.7 %all-gather.8.cloned.1.call-done = bf16[4096,512]{1,0:T(8,128)(2,1)} async-done(((bf16[128,512]{1,0:T(8,128)(2,1)}), bf16[4096,512]{1,0:T(8,128)(2,1)}) %all-gather.8.cloned.1.call-update) | async-done | bytes 4194320 | tf_op jit(solution)/shard_map/all_gather | solution.py:79
  185.8 48.4 %all-gather.6.cloned.1.call-done = bf16[512,4096]{0,1:T(8,128)(2,1)} async-done(((bf16[512,256]{0,1:T(8,128)(2,1)}), bf16[512,4096]{0,1:T(8,128)(2,1)}) %all-gather.6.cloned.1.call-update) | async-done | bytes 4194320 | tf_op jit(solution)/shard_map/all_gather | solution.py:76
  234.3 6.6 %fusion.3 = bf16[1,512,512]{2,1,0:T(8,128)(2,1)} fusion(bf16[512,4096]{0,1:T(8,128)(2,1)} %all-gather.6.cloned.1.call-done, bf16[4096,512]{1,0:T(8,128)(2,1)} %all-gather.8.cloned.1.call-done, bf16[1,512,512]{2,1,0:T(8,128)(2,1)S(1)} %copy-done.2), kind=kOutput, calls=%fused_computation.8 | convolution fusion | flops 2148270080 | bytes 9437184 | tf_op jit(solution)/shard_map/dot_general | solution.py:77
  (140 shorter events, 19.9 us)
Async XLA Ops:
  6.5 37.7 %copy-start = (bf16[1,512,256]{2,1,0:T(8,128)(2,1)S(1)}, bf16[1,512,256]{2,1,0:T(8,128)(2,1)}, u32[]{:S(2)}) copy-start(bf16[1,512,256]{2,1,0:T(8,128)(2,1)} %param.10) | copy-start | bytes 786436
  6.5 90.4 %all-gather.10.cloned.1.call-start = ((), (), s32[]{:S(2)}) async-start(), calls=%async_computation.2 | async-start | bytes 2162688 | tf_op jit(solution)/shard_map/all_gather | solution.py:12
  11.8 174.0 %all-gather.8.cloned.1.call-start = ((), (), s32[]{:S(2)}) async-start(), calls=%async_computation.1 | async-start | bytes 4325376 | tf_op jit(solution)/shard_map/all_gather | solution.py:79
  12.6 221.7 %all-gather.6.cloned.1.call-start = ((), (), s32[]{:S(2)}) async-start(), calls=%async_computation | async-start | bytes 4456448 | tf_op jit(solution)/shard_map/all_gather | solution.py:76
  134.2 1.1 copy-start.1
  134.2 100.1 %copy-start.2 = (bf16[1,512,512]{2,1,0:T(8,128)(2,1)S(1)}, bf16[1,512,512]{2,1,0:T(8,128)(2,1)}, u32[]{:S(2)}) copy-start(bf16[1,512,512]{2,1,0:T(8,128)(2,1)} %param.17) | copy-start | bytes 1572868
Sparse Core Ops, SparseCore 0:
  11.9 85.0 all-gather.9
  100.1 85.6 all-gather.7
  187.9 46.2 all-gather.5
where the time goes:
time: 249 us; the launch traced here: 247 us
  waiting for transfers between devices  152 us (61%)
  other arithmetic  33 us (13%)
  blocking collectives  31.4 us (13%)
  between operations  13.2 us (5%)
  matrix products  8.93 us (4%)
  local copies, waits for them, and re-layouts  8.36 us (3%)
    all_gather x1, waiting for transfers between devices, prefix_2(): lax.all_gather(part.astype(kind), axis)  52.7 us
    all_gather x1, waiting for transfers between devices, local(): lax.all_gather(out_weight, 'context', axis=0, tiled=True)  49.7 us
    all_gather x1, waiting for transfers between devices, local(): all_heads = lax.all_gather(normed, 'tensor', axis=1, tiled=True)  48.4 us
    all_gather x1, blocking collectives, prefix_2(): lax.all_gather(part.astype(kind), axis)  31.4 us
    select_n x32, other arithmetic, lap(): return jax.tree.map(lambda a, b: jnp.where(reached, a, b), new, before)  29.7 us
    dot_general x1, matrix products, local(): jnp.dot(all_heads, lax.all_gather(out_weight, 'context', axis=0, tiled=Tr...  6.61 us
    dynamic_slice x64, local copies, waits for them, and re-layouts, lap(): part[k].astype(own.dtype)  6.03 us
  transfers between devices with their start and end apart: 3, of which 3 were waited for; matrix products, arithmetic and copies ran while one was open for 16% of the time, Pallas kernels for 0%

commit v1 on v0

--- a/solution.py
+++ b/solution.py
@@ -1,9 +1,22 @@
+import functools
 import jax
 import jax.numpy as jnp
 from jax import lax
 from jax.sharding import PartitionSpec as P
 
 epsilon = 1e-06
+
+
+def list_lane(piece_in, axis_tag):
+    in_order = []
+    for _ in range(lax.axis_size(axis_tag)):
+        in_order.append(piece_in)
+    x_now = lax.all_to_all(jnp.stack(in_order), axis_name=axis_tag, split_axis=0, concat_axis=0)
+    now = jnp.concatenate(x_now, axis=1)
+    return now
+
+
+_watch_sites = functools.partial(list_lane, axis_tag="tensor")
 
 
 def prefix_2(value, axis, combine, identity):
@@ -73,7 +86,7 @@
     scale = lax.rsqrt(jnp.mean(mixed * mixed, axis=-1, keepdims=True) + epsilon)
     normed = (mixed * scale * norm_gain.reshape(1, heads, 1, head_size)).astype(jnp.bfloat16)
     normed = normed.transpose(0, 2, 1, 3).reshape(requests * block, width_here)
-    all_heads = lax.all_gather(normed, "tensor", axis=1, tiled=True)
+    all_heads = _watch_sites(normed)
     projected = jnp.dot(
         all_heads,
         lax.all_gather(out_weight, "context", axis=0, tiled=True),

time: 249 us -> 258 us (1.036)
  starting transfers between devices: 0.08 us -> 12 us
  waiting for transfers between devices: 152 us -> 147 us
    all_to_all x0 -> x1, waiting for transfers between devices: none -> 57.2 us  [list_lane(): lax.all_to_all(jnp.stack(in_order), axis_name=axis_tag, split_axis=0, con...]
    all_gather x1 -> x0, waiting for transfers between devices: 48.4 us -> none  [local(): all_heads = lax.all_gather(normed, 'tensor', axis=1, tiled=True)]
    all_gather x1, waiting for transfers between devices: 49.7 us -> 36.4 us  [local(): lax.all_gather(out_weight, 'context', axis=0, tiled=True)]
    all_to_all x0 -> x1, starting transfers between devices: none -> 12 us  [list_lane(): lax.all_to_all(jnp.stack(in_order), axis_name=axis_tag, split_axis=0, con...]
where the time goes in v1:
time: 258 us; the launch traced here: 257 us
  waiting for transfers between devices  147 us (57%)
  other arithmetic  32.3 us (13%)
  blocking collectives  31.4 us (12%)
  between operations  13.5 us (5%)
  starting transfers between devices  12 us (5%)
  local copies, waits for them, and re-layouts  10.7 us (4%)
  matrix products  8.95 us (3%)
    all_to_all x1, waiting for transfers between devices, list_lane(): lax.all_to_all(jnp.stack(in_order), axis_name=axis_tag, split_axis=0, con...  57.2 us
    all_gather x1, waiting for transfers between devices, prefix_2(): lax.all_gather(part.astype(kind), axis)  52.7 us
    all_gather x1, waiting for transfers between devices, local(): lax.all_gather(out_weight, 'context', axis=0, tiled=True)  36.4 us
    all_gather x1, blocking collectives, prefix_2(): lax.all_gather(part.astype(kind), axis)  31.4 us
    select_n x32, other arithmetic, lap(): return jax.tree.map(lambda a, b: jnp.where(reached, a, b), new, before)  29.7 us
    all_to_all x1, starting transfers between devices, list_lane(): lax.all_to_all(jnp.stack(in_order), axis_name=axis_tag, split_axis=0, con...  12 us
    dot_general x1, matrix products, local(): jnp.dot(all_heads, lax.all_gather(out_weight, 'context', axis=0, tiled=Tr...  6.61 us
    dynamic_slice x64, local copies, waits for them, and re-layouts, lap(): part[k].astype(own.dtype)  6.03 us
  transfers between devices with their start and end apart: 3, of which 3 were waited for; matrix products, arithmetic and copies ran while one was open for 16% of the time, Pallas kernels for 0%

profile of v1, /device:TPU:1, one launch (start us, length us, event | category | flops | bytes accessed | tf_op | source)
XLA Modules:
  0.0 256.5 jit_solution(4285925678293693236)
XLA Ops:
  8.4 1.1 multiply_convert_fusion.3
  9.5 1.1 copy.45
  12.7 31.4 %all-gather = bf16[32,2,1]{2,1,0:T(2,128)(2,1)S(1)} all-gather(bf16[1,2,1]{2,1,0:T(2,128)(2,1)S(1)} %get-tuple-element.154), channel_id=2, replica_groups=mesh['context'=32,'tensor'=16] {'context'}, dimensions={0}, use_global_device_ids=true | all-gather | bytes 132 | tf_op jit(solution)/shard_map/all_gather | solution.py:25
  44.2 52.7 %all-gather.7.cloned.1.call-done = bf16[64,128,128]{2,1,0:T(8,128)(2,1)} async-done(((bf16[2,128,128]{2,1,0:T(8,128)(2,1)}), bf16[64,128,128]{2,1,0:T(8,128)(2,1)}) %all-gather.7.cloned.1.call-update) | async-done | bytes 2097168 | tf_op jit(solution)/shard_map/all_gather | solution.py:25
  97.0 36.5 %while.14 = (s32[]{:T(128)}, f32[1,2,128,128]{3,2,1,0:T(8,128)S(1)}, s32[]{:T(128)}, bf16[32,1,2]{0,2,1:T(2,128)(2,1)S(1)}, bf16[32,1,2,128,128]{4,3,2,1,0:T(8,128)(2,1)}, /*index=5*/s32[]{:T(128)}, s32[]{:T(128)}) while((s32[]{:T(128)}, f32[1,2,128,128]{3,2,1,0:T(8,128)S(1)}, s32[]{:T(128)}, bf16[32,1,2]{0,2,1:T(2,128)(2,1)S(1)}, ...), condition=%wide.region_3.4_spmd.clone, body=%wide.region_2.3_spmd.clone.sunk | while | flops 163846 | bytes 327821 | solution.py:42
  99.5 0.9 fusion.25
  100.6 0.9 fusion.25
  101.7 0.9 fusion.25
  102.9 0.9 fusion.25
  104.0 0.9 fusion.25
  105.2 0.9 fusion.25
  106.3 0.9 fusion.25
  107.5 0.9 fusion.25
  115.4 0.9 fusion.25
  116.6 0.9 fusion.25
  117.7 0.9 fusion.25
  118.9 0.9 fusion.25
  120.0 0.9 fusion.25
  121.2 0.9 fusion.25
  122.3 0.9 fusion.25
  123.4 0.9 fusion.25
  125.7 0.9 fusion.25
  126.9 0.9 fusion.25
  128.0 0.9 fusion.25
  130.3 0.9 fusion.25
  131.4 0.9 fusion.25
  134.0 1.1 multiply_reduce_fusion
  135.1 2.4 stack.3
  137.5 12.0 %all-to-all-start = ((bf16[16,512,256]{1,2,0:T(8,128)(2,1)}), bf16[16,512,256]{1,2,0:T(8,128)(2,1)}, u32[]{:S(2)}, u32[]{:S(2)}) async-start(bf16[16,512,256]{1,2,0:T(8,128)(2,1)} %stack.3), calls=%async_computation | async-start | bytes 8388608 | tf_op jit(solution)/shard_map/all_to_all | solution.py:14
  149.5 36.4 %all-gather.5.cloned.1.call-done = bf16[4096,512]{1,0:T(8,128)(2,1)} async-done(((bf16[128,512]{1,0:T(8,128)(2,1)}), bf16[4096,512]{1,0:T(8,128)(2,1)}) %all-gather.5.cloned.1.call-update) | async-done | bytes 4194320 | tf_op jit(solution)/shard_map/all_gather | solution.py:92
  185.8 57.2 %all-to-all-done = bf16[16,512,256]{1,2,0:T(8,128)(2,1)} async-done(((bf16[16,512,256]{1,2,0:T(8,128)(2,1)}), bf16[16,512,256]{1,2,0:T(8,128)(2,1)}, u32[]{:S(2)}, u32[]{:S(2)}) %all-to-all-start) | async-done | bytes 4194336 | tf_op jit(solution)/shard_map/all_to_all | solution.py:14
  243.1 6.6 %fusion.3 = bf16[1,512,512]{2,1,0:T(8,128)(2,1)} fusion(bf16[512,4096]{0,1:T(8,128)(2,1)} %bitcast.17, bf16[4096,512]{1,0:T(8,128)(2,1)} %all-gather.5.cloned.1.call-done, bf16[1,512,512]{2,1,0:T(8,128)(2,1)S(1)} %copy-done.2), kind=kOutput, calls=%fused_computation.8 | convolution fusion | flops 2148270080 | bytes 9437184 | tf_op jit(solution)/shard_map/dot_general | solution.py:90
  (140 shorter events, 21.0 us)
Async XLA Ops:
  6.5 37.6 %copy-start = (bf16[1,512,256]{2,1,0:T(8,128)(2,1)S(1)}, bf16[1,512,256]{2,1,0:T(8,128)(2,1)}, u32[]{:S(2)}) copy-start(bf16[1,512,256]{2,1,0:T(8,128)(2,1)} %param.10) | copy-start | bytes 786436
  6.5 90.4 %all-gather.7.cloned.1.call-start = ((), (), s32[]{:S(2)}) async-start(), calls=%async_computation.2 | async-start | bytes 2162688 | tf_op jit(solution)/shard_map/all_gather | solution.py:25
  11.8 174.0 %all-gather.5.cloned.1.call-start = ((), (), s32[]{:S(2)}) async-start(), calls=%async_computation.1 | async-start | bytes 4325376 | tf_op jit(solution)/shard_map/all_gather | solution.py:92
  133.9 1.1 copy-start.1
  137.5 105.6 %copy-start.2 = (bf16[1,512,512]{2,1,0:T(8,128)(2,1)S(1)}, bf16[1,512,512]{2,1,0:T(8,128)(2,1)}, u32[]{:S(2)}) copy-start(bf16[1,512,512]{2,1,0:T(8,128)(2,1)} %param.17) | copy-start | bytes 1572868
  137.5 105.5 %all-to-all-start = ((bf16[16,512,256]{1,2,0:T(8,128)(2,1)}), bf16[16,512,256]{1,2,0:T(8,128)(2,1)}, u32[]{:S(2)}, u32[]{:S(2)}) async-start(bf16[16,512,256]{1,2,0:T(8,128)(2,1)} %stack.3), calls=%async_computation | async-start | bytes 8388608 | tf_op jit(solution)/shard_map/all_to_all | solution.py:14
Sparse Core Ops, SparseCore 0:
  11.9 85.0 all-gather.6
  100.1 85.6 all-gather.4
